TPU v7x, 512 devices: a whole 4x4x16 slice. The times are simulated.
512 devices in a mesh: grid: 64 (over z, y_hi, core), orb: 8 (over y_lo, x).
Axes of the slice: x: 4, y: 4 (y_hi: 2, y_lo: 2; y = y_hi * 2 + y_lo), z: 16, core: 2. Of those that a mesh axis runs over, the one named last changes fastest.
Arguments:
- orbitals: bfloat16 [16384, 8192], P('grid', 'orb'), may hold values from -6 to 6
- points: int32 [4096], P('grid'), may hold values from 0 to 16383, as said below
Outputs:
- fitted: float32 [16384, 4096], P('grid', 'orb')
- gram: float32 [4096, 4096], P('grid', 'orb')
- density: float32 [4096], P('grid')
Inputs may be any that keep to these rules, and one draw needn't show every extreme that they name: `points`: entries 64 * g to 64 * g + 63 are distinct grid rows of slab g, the rows 256 * g to 256 * g + 255.
All inputs are finite; a program needn't handle non-finite values.
Results may differ from a plain program's by a relative error of at most 0.0003.
Values may be sent and summed in bfloat16 or wider, within the bound.
No kernel may reach another device: no remote copies, remote signals or barrier semaphores. Data moves between devices by JAX's collectives and lax.ppermute only.
A program may use at most 64 MiB of HBM per device.

v0:
```python
import jax
import jax.numpy as jnp
from jax import lax
from jax.sharding import Mesh
from jax.sharding import PartitionSpec as P

NORB = 8192
GRID = ("grid_0", "grid_1", "grid_2")


def joined_along(pieces, dim):
    pieces = jnp.moveaxis(pieces, 0, dim)
    shape = pieces.shape
    return pieces.reshape(*shape[:dim], shape[dim] * shape[dim + 1], *shape[dim + 2 :])


def all_blocks(value, axes, turns):
    pieces = value[None]
    for k in turns:
        pieces = lax.all_gather(pieces, axes[k], axis=0, tiled=True)
    current = [lax.axis_size(axes[k]) for k in reversed(turns)]
    pieces = pieces.reshape(*current, *value.shape)
    turned = sorted(range(len(turns)), key=lambda place: turns[len(turns) - 1 - place])
    return pieces.transpose(*turned, *range(len(turns), pieces.ndim)).reshape(-1, *value.shape)


def whole_of(value, axes, turns, dim):
    return joined_along(all_blocks(value, axes, turns), dim)


def side_by_side(arrays, axis, dim, along):
    widths = [a.shape[along] for a in arrays]
    both = jnp.concatenate(arrays, axis=along)
    whole = lax.psum_scatter(both, axis, scatter_dimension=dim, tiled=True)
    return tuple(jnp.split(whole, [sum(widths[:k]) for k in range(1, len(widths))], axis=along))


def sent_to_all(value, axis):
    copies = jnp.broadcast_to(value, (lax.axis_size(axis), *value.shape))
    return lax.all_to_all(copies, axis, split_axis=0, concat_axis=0, tiled=True)


def over_copies(value, axis):
    return sent_to_all(value, axis).sum(axis=0)


def contract(left, right):
    return lax.dot_general(
        left, right, (((1,), (1,)), ((), ())), preferred_element_type=jnp.float32
    )


def on_device(orbitals, points):
    rows = orbitals.shape[0]
    mu_dev = points.shape[0]
    total_mu = mu_dev * lax.axis_size(GRID)
    slab_start = lax.axis_index(GRID) * rows
    local_rows = points - slab_start
    chosen = jnp.take(orbitals, local_rows, axis=0)
    chosen_wide = chosen.astype(jnp.float32)
    dens_part = jnp.sum(chosen_wide * chosen_wide, axis=1)
    every = whole_of(chosen, GRID, (1, 0, 2), 0)
    pair = contract(orbitals, every)
    correlation = contract(chosen, every)
    width = total_mu // lax.axis_size("orb")
    col_start = lax.axis_index("orb") * width
    pair_share, over_share = side_by_side((pair, correlation), "orb", 1, 0)
    dens_all = over_copies(dens_part, "orb")
    scale = 1.0 / jnp.sqrt(jnp.float32(NORB))
    fitted = jnp.square(pair_share * scale)
    row_ids = lax.axis_index(GRID) * mu_dev + jnp.arange(mu_dev, dtype=jnp.int32)
    col_ids = col_start + jnp.arange(width, dtype=jnp.int32)
    diagonal_mask = row_ids[:, None] == col_ids[None, :]
    gram = jnp.where(diagonal_mask, jnp.float32(0.0), jnp.square(over_share * scale))
    density = dens_all / jnp.float32(NORB)
    return (fitted, gram, density)


def solution(mesh):
    torus = Mesh(
        mesh.devices.reshape(16, 2, 2, mesh.shape["orb"]), ("grid_0", "grid_1", "grid_2", "orb")
    )
    in_specs = (P(GRID, "orb"), P(GRID))
    out_specs = (P(GRID, "orb"), P(GRID, "orb"), P(GRID))
    return jax.shard_map(
        on_device, mesh=torus, in_specs=in_specs, out_specs=out_specs, check_vma=False
    )
```

profile of v0, /device:TPU:1, one launch (start us, length us, event | category | flops | bytes accessed | tf_op | source)
XLA Modules:
  0.0 230.9 jit_solution(3871971614468897059)
XLA Ops:
  7.2 0.0 copy-start
  7.2 0.0 all-gather.3.cloned.1.call-start
  7.2 0.7 compare_and_fusion
  8.0 0.3 copy-done
  8.2 0.7 gather_fusion
  8.9 0.1 bitcast_select_fusion
  9.0 6.8 %all_gather.9 = bf16[2,64,1024]{2,1,0:T(8,128)(2,1)} all-gather(bf16[1,64,1024]{2,1,0:T(8,128)(2,1)S(1)} %bitcast_select_fusion), channel_id=1, replica_groups=mesh['grid_0'=16,'grid_1'=2,'grid_2'=2,'orb'=8] {'grid_1'}, dimensions={0}, use_global_device_ids=true | all-gather | bytes 393216 | tf_op jit(solution)/shard_map/all_gather | solution.py:20
  15.9 0.0 all-gather.3.cloned.1.call-update
  15.9 0.0 all-gather.5.cloned.1.call-start
  15.9 75.3 %all-gather.3.cloned.1.call-done = bf16[32,64,1024]{2,1,0:T(8,128)(2,1)} async-done(((bf16[2,64,1024]{2,1,0:T(8,128)(2,1)}), bf16[32,64,1024]{2,1,0:T(8,128)(2,1)}) %all-gather.3.cloned.1.call-update) | async-done | bytes 4194320 | tf_op jit(solution)/shard_map/all_gather | solution.py:20
  91.2 0.0 all-gather.5.cloned.1.call-update
  91.3 0.0 reduce-scatter.2.cloned.1.call-start
  91.3 39.0 %all-gather.5.cloned.1.call-done = bf16[64,64,1024]{2,1,0:T(8,128)(2,1)} async-done(((bf16[32,64,1024]{2,1,0:T(8,128)(2,1)}), bf16[64,64,1024]{2,1,0:T(8,128)(2,1)}) %all-gather.5.cloned.1.call-update) | async-done | bytes 8388624 | tf_op jit(solution)/shard_map/all_gather | solution.py:20
  130.3 8.4 %copy.8 = bf16[16,2,2,64,1024]{4,3,2,1,0:T(8,128)(2,1)} copy(bf16[16,2,2,64,1024]{4,3,1,0,2:T(8,128)(2,1)} %bitcast.14) | data formatting | bytes 16777216 | tf_op jit(solution)/shard_map/transpose | solution.py:24
  138.7 0.0 copy-start.1
  138.7 6.2 %fusion.3 = f32[64,4096]{1,0:T(8,128)S(1)} fusion(bf16[4096,1024]{1,0:T(8,128)(2,1)} %bitcast.12, bf16[64,1024]{1,0:T(8,128)(2,1)S(1)} %gather_fusion, pred[64]{0:T(512)(128)(4,1)S(1)} %get-tuple-element.3), kind=kOutput, calls=%fused_computation.11 | convolution fusion | flops 536936448 | bytes 9568320 | tf_op jit(solution)/shard_map/dot_general | solution.py:48
  144.9 0.0 copy-done.1
  144.9 2.4 %convolution_bitcast_fusion = f32[256,4096]{1,0:T(8,128)S(1)} fusion(bf16[4096,1024]{1,0:T(8,128)(2,1)S(1)} %bitcast.13, bf16[256,1024]{1,0:T(8,128)(2,1)S(1)} %copy-done), kind=kOutput, calls=%fused_computation.1 | convolution fusion | flops 2147483648 | bytes 13107200 | tf_op jit(solution)/shard_map/dot_general | solution.py:48
  147.3 2.9 %pad_maximum_fusion = f32[320,4096]{1,0:T(8,128)} fusion(f32[64,4096]{1,0:T(8,128)S(1)} %fusion.3, f32[256,4096]{1,0:T(8,128)S(1)} %convolution_bitcast_fusion), kind=kLoop, calls=%fused_computation.2 | loop fusion | flops 1310720 | bytes 10485760 | tf_op jit(solution)/shard_map/concatenate | solution.py:33
  150.2 0.0 reduce-scatter.2.cloned.1.call-update
  150.2 0.2 multiply_reduce_fusion
  150.4 0.6 broadcast_in_dim.32
  151.0 3.9 %all-to-all-start = ((f32[8,1,64]{2,1,0:T(1,128)}), f32[8,1,64]{2,1,0:T(1,128)S(1)}, u32[]{:S(2)}, u32[]{:S(2)}) async-start(f32[8,1,64]{2,1,0:T(1,128)} %broadcast_in_dim.32), calls=%async_computation.1 | async-start | bytes 8192 | tf_op jit(solution)/shard_map/all_to_all | solution.py:40
  154.9 4.9 %all-to-all-done = f32[8,1,64]{2,1,0:T(1,128)S(1)} async-done(((f32[8,1,64]{2,1,0:T(1,128)}), f32[8,1,64]{2,1,0:T(1,128)S(1)}, u32[]{:S(2)}, u32[]{:S(2)}) %all-to-all-start) | async-done | bytes 2080 | tf_op jit(solution)/shard_map/all_to_all | solution.py:40
  159.9 0.5 broadcast_multiply_fusion
  160.4 60.4 %reduce-scatter.2.cloned.1.call-done = f32[320,512]{1,0:T(8,128)} async-done(((f32[320,4096]{1,0:T(8,128)}), f32[320,512]{1,0:T(8,128)}) %reduce-scatter.2.cloned.1.call-update) | async-done | bytes 655376 | tf_op jit(solution)/shard_map/reduce_scatter | solution.py:34
  220.8 1.9 fusion
  222.7 1.6 fusion.2
  (4 shorter events, 0.0 us)
Async XLA Ops:
  7.2 1.1 copy-start
  7.2 84.1 %all-gather.3.cloned.1.call-start = ((), (), s32[]{:S(2)}) async-start(), calls=%async_computation.2 | async-start | bytes 4456448 | tf_op jit(solution)/shard_map/all_gather | solution.py:20
  15.9 114.4 %all-gather.5.cloned.1.call-start = ((), (), s32[]{:S(2)}) async-start(), calls=%async_computation.3 | async-start | bytes 12582912 | tf_op jit(solution)/shard_map/all_gather | solution.py:20
  91.3 129.6 %reduce-scatter.2.cloned.1.call-start = ((), (), s32[]{:S(2)}) async-start(), calls=%async_computation.4 | async-start | bytes 5898240 | tf_op jit(solution)/shard_map/reduce_scatter | solution.py:34
  138.7 6.2 %copy-start.1 = (bf16[16,2,2,64,1024]{4,3,2,1,0:T(8,128)(2,1)S(1)}, bf16[16,2,2,64,1024]{4,3,2,1,0:T(8,128)(2,1)}, u32[]{:S(2)}) copy-start(bf16[16,2,2,64,1024]{4,3,2,1,0:T(8,128)(2,1)} %copy.8) | copy-start | bytes 25165828
  151.0 8.9 %all-to-all-start = ((f32[8,1,64]{2,1,0:T(1,128)}), f32[8,1,64]{2,1,0:T(1,128)S(1)}, u32[]{:S(2)}, u32[]{:S(2)}) async-start(f32[8,1,64]{2,1,0:T(1,128)} %broadcast_in_dim.32), calls=%async_computation.1 | async-start | bytes 8192 | tf_op jit(solution)/shard_map/all_to_all | solution.py:40
Sparse Core Ops, SparseCore 0:
  16.0 75.1 all-gather.2
  93.3 36.9 all-gather.4
  150.3 70.4 reduce-scatter.1
where the time goes:
time: 231 us
  waiting for transfers between devices  180 us (78%)
  between operations  13.8 us (6%)
  local copies, waits for them, and re-layouts  9.99 us (4%)
  matrix products  8.59 us (4%)
  other arithmetic  7.93 us (3%)
  blocking collectives  6.85 us (3%)
  starting transfers between devices  4.01 us (2%)
    all_gather x2, waiting for transfers between devices, all_blocks(): pieces = lax.all_gather(pieces, axes[k], axis=0, tiled=True)  114 us
    reduce_scatter x1, waiting for transfers between devices, side_by_side(): whole = lax.psum_scatter(both, axis, scatter_dimension=dim, tiled=True)  60.4 us
    dot_general x2, matrix products, contract(): lax.dot_general(left, right, (((1,), (1,)), ((), ())), preferred_element_...  8.59 us
    transpose x1, local copies, waits for them, and re-layouts, all_blocks(): pieces.transpose(*turned, *range(len(turns), pieces.ndim))  8.4 us
    all_gather x1, blocking collectives, all_blocks(): pieces = lax.all_gather(pieces, axes[k], axis=0, tiled=True)  6.85 us
    all_to_all x1, waiting for transfers between devices, sent_to_all(): return lax.all_to_all(copies, axis, split_axis=0, concat_axis=0, tiled=True)  4.94 us
  transfers between devices with their start and end apart: 4, of which 4 were waited for; matrix products, arithmetic and copies ran while one was open for 1% of the time, Pallas kernels for 0%

commit v1 on v0

--- a/solution.py
+++ b/solution.py
@@ -17,7 +17,9 @@
 def all_blocks(value, axes, turns):
     pieces = value[None]
     for k in turns:
-        pieces = lax.all_gather(pieces, axes[k], axis=0, tiled=True)
+        pieces = jnp.concatenate(
+            lax.all_to_all(jnp.stack([pieces] * lax.axis_size(axes[k])), axes[k], 0, 0), axis=0
+        )
     current = [lax.axis_size(axes[k]) for k in reversed(turns)]
     pieces = pieces.reshape(*current, *value.shape)
     turned = sorted(range(len(turns)), key=lambda place: turns[len(turns) - 1 - place])

time: 231 us -> 339 us (1.47)
  blocking collectives: 6.85 us -> 230 us
  waiting for transfers between devices: 180 us -> 59.1 us
  other arithmetic: 7.93 us -> 11.9 us
    all_to_all x0 -> x3, blocking collectives: none -> 230 us  [all_blocks(): lax.all_to_all(jnp.stack([pieces] * lax.axis_size(axes[k])), axes[k], 0, 0)]
    all_gather x2 -> x0, waiting for transfers between devices: 114 us -> none  [all_blocks(): pieces = lax.all_gather(pieces, axes[k], axis=0, tiled=True)]
    transpose x1 -> x0, local copies, waits for them, and re-layouts: 8.4 us -> none  [all_blocks(): pieces.transpose(*turned, *range(len(turns), pieces.ndim))]
    all_to_all x0 -> x1, local copies, waits for them, and re-layouts: none -> 8.39 us  [all_blocks(): lax.all_to_all(jnp.stack([pieces] * lax.axis_size(axes[k])), axes[k], 0, 0)]
    all_gather x1 -> x0, blocking collectives: 6.85 us -> none  [all_blocks(): pieces = lax.all_gather(pieces, axes[k], axis=0, tiled=True)]
    reduce_scatter x1, waiting for transfers between devices: 60.4 us -> 54.1 us  [side_by_side(): whole = lax.psum_scatter(both, axis, scatter_dimension=dim, tiled=True)]
    another operation x0 -> x2, other arithmetic: none -> 3.95 us  [all_blocks(): jnp.stack([pieces] * lax.axis_size(axes[k]))]
  transfers between devices with their start and end apart: 4 -> 2, of which waited for: 4 -> 2; matrix products, arithmetic and copies ran while one was open for 1% -> 0% of each run, Pallas kernels for 0% -> 0%
where the time goes in v1:
time: 339 us; the launch traced here: 338 us
  blocking collectives  230 us (68%)
  waiting for transfers between devices  59.1 us (17%)
  between operations  14.1 us (4%)
  other arithmetic  11.9 us (4%)
  local copies, waits for them, and re-layouts  10.5 us (3%)
  matrix products  8.6 us (3%)
  starting transfers between devices  4.17 us (1%)
    all_to_all x3, blocking collectives, all_blocks(): lax.all_to_all(jnp.stack([pieces] * lax.axis_size(axes[k])), axes[k], 0, 0)  230 us
    reduce_scatter x1, waiting for transfers between devices, side_by_side(): whole = lax.psum_scatter(both, axis, scatter_dimension=dim, tiled=True)  54.1 us
    dot_general x2, matrix products, contract(): lax.dot_general(left, right, (((1,), (1,)), ((), ())), preferred_element_...  8.6 us
    all_to_all x1, local copies, waits for them, and re-layouts, all_blocks(): lax.all_to_all(jnp.stack([pieces] * lax.axis_size(axes[k])), axes[k], 0, 0)  8.39 us
  transfers between devices with their start and end apart: 2, of which 2 were waited for; matrix products, arithmetic and copies ran while one was open for 0% of the time, Pallas kernels for 0%

profile of v1, /device:TPU:1, one launch (start us, length us, event | category | flops | bytes accessed | tf_op | source)
XLA Modules:
  0.0 338.0 jit_solution(697026133427491118)
XLA Ops:
  7.2 0.0 copy-start
  7.2 0.0 reduce-scatter.2.cloned.1.call-start
  7.2 0.7 compare_and_fusion
  8.0 0.3 copy-done
  8.2 0.7 gather_fusion
  8.9 0.1 bitcast_select_fusion
  9.0 10.3 %all_to_all.21 = bf16[2,1,64,1024]{3,2,1,0:T(8,128)(2,1)S(1)} all-to-all(bf16[2,1,64,1024]{3,2,1,0:T(8,128)(2,1)S(1)} %pad_maximum_fusion.2), channel_id=1, replica_groups=mesh['grid_0'=16,'grid_1'=2,'grid_2'=2,'orb'=8] {'grid_1'}, dimensions={0} | all-to-all | bytes 524288 | tf_op jit(solution)/shard_map/all_to_all | solution.py:21
  19.4 0.5 stack.10
  19.9 194.1 %all_to_all.22 = bf16[16,2,64,1024]{3,2,1,0:T(8,128)(2,1)S(1)} all-to-all(bf16[16,2,64,1024]{3,2,1,0:T(8,128)(2,1)S(1)} %stack.10), channel_id=1, replica_groups=mesh['grid_0'=16,'grid_1'=2,'grid_2'=2,'orb'=8] {'grid_0'}, dimensions={0} | all-to-all | bytes 8388608 | tf_op jit(solution)/shard_map/all_to_all | solution.py:21
  214.0 3.9 %pad_maximum_fusion = bf16[2,32,64,1024]{3,2,1,0:T(8,128)(2,1)} fusion(bf16[1,32,64,1024]{3,2,1,0:T(8,128)(2,1)S(1)} %bitcast.17), kind=kLoop, calls=%fused_computation.1 | loop fusion | flops 4194304 | bytes 12582912 | tf_op jit(solution)/shard_map/stack | solution.py:21
  217.9 25.2 %all_to_all.23 = bf16[2,32,64,1024]{3,2,1,0:T(8,128)(2,1)} all-to-all(bf16[2,32,64,1024]{3,2,1,0:T(8,128)(2,1)} %pad_maximum_fusion), channel_id=1, replica_groups=mesh['grid_0'=16,'grid_1'=2,'grid_2'=2,'orb'=8] {'grid_2'}, dimensions={0} | all-to-all | bytes 16777216 | tf_op jit(solution)/shard_map/all_to_all | solution.py:21
  243.1 8.4 %copy.7 = bf16[2,32,64,1024]{3,2,0,1:T(8,128)(2,1)} copy(bf16[2,32,64,1024]{3,2,1,0:T(8,128)(2,1)} %all_to_all.23) | data formatting | bytes 16777216 | tf_op jit(solution)/shard_map/all_to_all | solution.py:21
  251.5 0.0 copy-start.1
  251.5 6.2 %fusion.3 = f32[64,4096]{1,0:T(8,128)S(1)} fusion(bf16[4096,1024]{1,0:T(8,128)(2,1)} %bitcast.15, bf16[64,1024]{1,0:T(8,128)(2,1)S(1)} %gather_fusion, pred[64]{0:T(512)(128)(4,1)S(1)} %get-tuple-element.3), kind=kOutput, calls=%fused_computation.13 | convolution fusion | flops 536936448 | bytes 9568320 | tf_op jit(solution)/shard_map/dot_general | solution.py:50
  257.7 0.0 copy-done.1
  257.8 2.4 convolution_bitcast_fusion
  260.2 2.9 pad_maximum_fusion.1
  263.0 0.0 reduce-scatter.2.cloned.1.call-update
  263.1 0.2 multiply_reduce_fusion
  263.3 0.6 broadcast_in_dim.31
  263.9 4.1 %all-to-all-start.3 = ((f32[8,1,64]{2,1,0:T(1,128)}), f32[8,1,64]{2,1,0:T(1,128)S(1)}, u32[]{:S(2)}, u32[]{:S(2)}) async-start(f32[8,1,64]{2,1,0:T(1,128)} %broadcast_in_dim.31), calls=%async_computation.4 | async-start | bytes 8192 | tf_op jit(solution)/shard_map/all_to_all | solution.py:42
  268.0 4.9 %all-to-all-done.3 = f32[8,1,64]{2,1,0:T(1,128)S(1)} async-done(((f32[8,1,64]{2,1,0:T(1,128)}), f32[8,1,64]{2,1,0:T(1,128)S(1)}, u32[]{:S(2)}, u32[]{:S(2)}) %all-to-all-start.3) | async-done | bytes 2080 | tf_op jit(solution)/shard_map/all_to_all | solution.py:42
  273.0 0.5 broadcast_multiply_fusion
  273.5 54.1 %reduce-scatter.2.cloned.1.call-done = f32[320,512]{1,0:T(8,128)} async-done(((f32[320,4096]{1,0:T(8,128)}), f32[320,512]{1,0:T(8,128)}) %reduce-scatter.2.cloned.1.call-update) | async-done | bytes 655376 | tf_op jit(solution)/shard_map/reduce_scatter | solution.py:36
  327.6 1.9 fusion
  329.5 1.6 fusion.2
  (5 shorter events, 0.1 us)
Async XLA Ops:
  7.2 1.1 copy-start
  7.2 320.4 %reduce-scatter.2.cloned.1.call-start = ((), (), s32[]{:S(2)}) async-start(), calls=%async_computation.5 | async-start | bytes 5898240 | tf_op jit(solution)/shard_map/reduce_scatter | solution.py:36
  251.5 6.2 %copy-start.1 = (bf16[2,32,64,1024]{3,2,0,1:T(8,128)(2,1)S(1)}, bf16[2,32,64,1024]{3,2,0,1:T(8,128)(2,1)}, u32[]{:S(2)}) copy-start(bf16[2,32,64,1024]{3,2,0,1:T(8,128)(2,1)} %copy.7) | copy-start | bytes 25165828
  263.9 9.1 %all-to-all-start.3 = ((f32[8,1,64]{2,1,0:T(1,128)}), f32[8,1,64]{2,1,0:T(1,128)S(1)}, u32[]{:S(2)}, u32[]{:S(2)}) async-start(f32[8,1,64]{2,1,0:T(1,128)} %broadcast_in_dim.31), calls=%async_computation.4 | async-start | bytes 8192 | tf_op jit(solution)/shard_map/all_to_all | solution.py:42
Sparse Core Ops, SparseCore 0:
  263.2 64.3 reduce-scatter.1
